TPU v7x, 512 devices: a whole 4x8x8 slice. The times are simulated.
512 devices in a mesh: dp: 4 (over y_lo), fsdp: 32 (over x, z), head: 4 (over y_hi, core).
Axes of the slice: x: 4, y: 8 (y_hi: 2, y_lo: 4; y = y_hi * 4 + y_lo), z: 8, core: 2. Of those that a mesh axis runs over, the one named last changes fastest.
Arguments:
- queries: bfloat16 [4, 8192, 2048], P('dp', 'fsdp', 'head'), may hold values from -8 to 8
- key_rows: bfloat16 [4, 8192, 2048], P('dp', 'fsdp', 'head'), may hold values from -8 to 8
- value_rows: bfloat16 [4, 8192, 2048], P('dp', 'fsdp', 'head'), may hold values from -6 to 6
- out_weight: bfloat16 [2048, 2048], P('fsdp', 'head'), may hold values from -0.125 to 0.125
- sum_lists: int32 [4, 64, 16], P('dp', 'fsdp'), may hold values from 0 to 31, as said below
- out_grad: bfloat16 [4, 8192, 2048], P('dp', 'fsdp', 'head'), may hold values from -6 to 6
Outputs:
- projected: bfloat16 [4, 8192, 2048], P('dp', 'fsdp', 'head')
- query_grad: bfloat16 [4, 8192, 2048], P('dp', 'fsdp', 'head')
- key_grad: bfloat16 [4, 8192, 2048], P('dp', 'fsdp', 'head')
- value_grad: bfloat16 [4, 8192, 2048], P('dp', 'fsdp', 'head')
- weight_grad: float32 [2048, 2048], P('fsdp', 'head')
Inputs may be any that keep to these rules, and one draw needn't show every extreme that they name: `sum_lists`: each row names 16 different strides.
All inputs are finite; a program needn't handle non-finite values.
Results may differ from a plain program's by a relative error of at most 0.028.
Values may be sent and summed in bfloat16 or wider, within the bound.
A program may use at most 64 MiB of HBM per device.

v0:
```python
from functools import reduce
import math
import jax
import jax.numpy as jnp
from jax import lax
from jax.sharding import PartitionSpec as P

HS = 128
BLK = 128
WIN = 3
STRIDE = 256
SUMC = 8


def shifted(block, axis, distance):
    devices = range(lax.axis_size(axis))
    route = [(i - distance, i) for i in devices if i - distance in devices]
    return lax.ppermute(block, axis, route)


def masked_softmax(scores, allowed):
    scores = jnp.where(allowed[:, None], scores, -jnp.inf)
    peak = jnp.max(scores, axis=3, keepdims=True)
    raised = jnp.exp(scores - peak)
    return raised / jnp.sum(raised, axis=3, keepdims=True)


def window_blocks(prior, current, blocks):
    width = current.shape[1]
    joined = jnp.concatenate([prior, current], axis=0).reshape(blocks + WIN - 1, BLK, width)
    stacked = jnp.stack([joined[offset : offset + blocks] for offset in range(WIN)], axis=1)
    return stacked.reshape(blocks, WIN * BLK, width)


def fold_window(grad_keys, blocks):
    width = grad_keys.shape[2]
    nearby = grad_keys[:, : WIN * BLK].reshape(blocks, WIN, BLK, width)
    placed = [
        jnp.pad(nearby[:, offset], ((offset, WIN - 1 - offset), (0, 0), (0, 0)))
        for offset in range(WIN)
    ]
    return reduce(jnp.add, placed).reshape((blocks + WIN - 1) * BLK, width)


def owner_rows(grad_keys, selector, fsdp_count, stride_count):
    blocks = grad_keys.shape[0]
    width = grad_keys.shape[2]
    distant = grad_keys[:, WIN * BLK :].reshape(blocks, selector.shape[1], SUMC * width)
    summed = jnp.einsum("bsn,bsc->nc", selector, distant, precision=lax.Precision.HIGHEST)
    return summed.reshape(fsdp_count, stride_count * SUMC, width)


def body(queries, key_rows, value_rows, out_weight, sum_lists, out_grad):
    query_tok = queries[0]
    key_tok = key_rows[0]
    value_tok = value_rows[0]
    grad_tok = out_grad[0]
    chosen = sum_lists[0]
    fsdp_count = lax.axis_size("fsdp")
    fsdp_pos = lax.axis_index("fsdp")
    tokens = query_tok.shape[0]
    width = query_tok.shape[1]
    head_count = width // HS
    blocks = tokens // BLK
    stride_count = tokens // STRIDE
    summary_count = stride_count * fsdp_count
    pick_count = chosen.shape[1]
    margin = (WIN - 1) * BLK
    score_scale = 1.0 / math.sqrt(HS)
    prior_keys, prior_values = shifted((key_tok, value_tok), "fsdp", 1)
    tail_keys = key_tok.reshape(stride_count, STRIDE, width)[:, STRIDE - SUMC :]
    tail_values = value_tok.reshape(stride_count, STRIDE, width)[:, STRIDE - SUMC :]
    summary_keys, summary_values = (
        lax.all_gather(tail_keys, "fsdp", axis=0, tiled=True),
        lax.all_gather(tail_values, "fsdp", axis=0, tiled=True),
    )
    far_keys = summary_keys[chosen].reshape(blocks, pick_count * SUMC, width)
    far_values = summary_values[chosen].reshape(blocks, pick_count * SUMC, width)
    block_keys = jnp.concatenate(
        [window_blocks(prior_keys, key_tok, blocks), far_keys], axis=1
    ).reshape(blocks, -1, head_count, HS)
    block_values = jnp.concatenate(
        [window_blocks(prior_values, value_tok, blocks), far_values], axis=1
    ).reshape(blocks, -1, head_count, HS)
    block_queries = query_tok.reshape(blocks, BLK, head_count, HS)
    block_ids = fsdp_pos * blocks + jnp.arange(blocks, dtype=jnp.int32)
    query_pos = block_ids[:, None] * BLK + jnp.arange(BLK, dtype=jnp.int32)[None, :]
    window_start = (block_ids - WIN + 1) * BLK
    key_pos = window_start[:, None] + jnp.arange(WIN * BLK, dtype=jnp.int32)[None, :]
    nearby_ok = (key_pos[:, None, :] >= 0) & (key_pos[:, None, :] <= query_pos[:, :, None])
    distant_ok = jnp.repeat((chosen + 1) * STRIDE <= window_start[:, None], SUMC, axis=1)
    allowed = jnp.concatenate(
        [nearby_ok, jnp.broadcast_to(distant_ok[:, None, :], (blocks, BLK, pick_count * SUMC))],
        axis=2,
    )
    scores = (
        jnp.einsum("bihd,bjhd->bhij", block_queries, block_keys, preferred_element_type=jnp.float32)
        * score_scale
    )
    weights = masked_softmax(scores, allowed)
    weights_b = weights.astype(jnp.bfloat16)
    mixed = jnp.einsum(
        "bhij,bjhd->bihd", weights_b, block_values, preferred_element_type=jnp.float32
    )
    mixed = mixed.reshape(tokens, width).astype(jnp.bfloat16)
    all_mixed = lax.all_gather(mixed, "head", axis=1, tiled=True)
    weight_cols = lax.all_gather(out_weight, "fsdp", axis=0, tiled=True)
    projected = jnp.dot(all_mixed, weight_cols, preferred_element_type=jnp.float32).astype(
        jnp.bfloat16
    )
    grad_all = lax.all_gather(grad_tok, "head", axis=1, tiled=True)
    weight_all = lax.all_to_all(weight_cols, "head", split_axis=0, concat_axis=1, tiled=True)
    grad_mixed = lax.dot_general(
        grad_all, weight_all, (((1,), (1,)), ((), ())), preferred_element_type=jnp.float32
    ).astype(jnp.bfloat16)
    grad_blocks = grad_mixed.reshape(blocks, BLK, head_count, HS)
    delta = jnp.sum(
        grad_blocks.astype(jnp.float32)
        * mixed.reshape(blocks, BLK, head_count, HS).astype(jnp.float32),
        axis=3,
    )
    delta = jnp.transpose(delta, (0, 2, 1))[:, :, :, None]
    dprob = jnp.einsum(
        "bihd,bjhd->bhij", grad_blocks, block_values, preferred_element_type=jnp.float32
    )
    dscore = (weights * (dprob - delta)).astype(jnp.bfloat16)
    query_grad = (
        jnp.einsum("bhij,bjhd->bihd", dscore, block_keys, preferred_element_type=jnp.float32)
        * score_scale
    )
    query_grad = query_grad.reshape(tokens, width).astype(jnp.bfloat16)
    key_terms = (
        jnp.einsum("bhij,bihd->bjhd", dscore, block_queries, preferred_element_type=jnp.float32)
        * score_scale
    ).reshape(blocks, -1, width)
    value_terms = jnp.einsum(
        "bhij,bihd->bjhd", weights_b, grad_blocks, preferred_element_type=jnp.float32
    ).reshape(blocks, -1, width)
    key_window = fold_window(key_terms, blocks)
    value_window = fold_window(value_terms, blocks)
    back_keys, back_values = (
        shifted(key_window[:margin].astype(jnp.bfloat16), "fsdp", -1).astype(jnp.float32),
        shifted(value_window[:margin].astype(jnp.bfloat16), "fsdp", -1).astype(jnp.float32),
    )
    selector = (
        chosen[:, :, None] == jnp.arange(summary_count, dtype=jnp.int32)[None, None, :]
    ).astype(jnp.float32)
    got_keys, got_values = (
        lax.all_to_all(
            owner_rows(key_terms, selector, fsdp_count, stride_count).astype(jnp.bfloat16),
            "fsdp",
            split_axis=0,
            concat_axis=0,
            tiled=True,
        ).astype(jnp.float32),
        lax.all_to_all(
            owner_rows(value_terms, selector, fsdp_count, stride_count).astype(jnp.bfloat16),
            "fsdp",
            split_axis=0,
            concat_axis=0,
            tiled=True,
        ).astype(jnp.float32),
    )

    def finish(window_rows, back_rows, owner_got):
        own_rows = window_rows[margin:]
        own_rows = jnp.concatenate([own_rows[: tokens - margin], own_rows + back_rows], axis=0)
        owner_sum = jnp.sum(owner_got, axis=0).reshape(stride_count, SUMC, width)
        own_rows = own_rows.reshape(stride_count, STRIDE, width)
        own_rows = jnp.concatenate(
            [own_rows[:, : STRIDE - SUMC], own_rows[:, STRIDE - SUMC :] + owner_sum], axis=1
        )
        return own_rows.reshape(tokens, width).astype(jnp.bfloat16)

    key_grad = finish(key_window, back_keys, got_keys)
    value_grad = finish(value_window, back_values, got_values)
    shard_rows = lax.psum_scatter(
        lax.dot_general(
            all_mixed, grad_tok, (((0,), (0,)), ((), ())), preferred_element_type=jnp.float32
        ).astype(jnp.bfloat16),
        "fsdp",
        scatter_dimension=0,
        tiled=True,
    )
    weight_grad = lax.psum(shard_rows, "dp").astype(jnp.float32)
    return (projected[None], query_grad[None], key_grad[None], value_grad[None], weight_grad)


def solution(mesh):
    placed = (
        P("dp", "fsdp", "head"),
        P("dp", "fsdp", "head"),
        P("dp", "fsdp", "head"),
        P("fsdp", "head"),
        P("dp", "fsdp", None),
        P("dp", "fsdp", "head"),
    )
    return jax.shard_map(
        body,
        mesh=mesh,
        in_specs=placed,
        out_specs=(
            P("dp", "fsdp", "head"),
            P("dp", "fsdp", "head"),
            P("dp", "fsdp", "head"),
            P("dp", "fsdp", "head"),
            P("fsdp", "head"),
        ),
        check_vma=False,
    )
```

profile of v0, /device:TPU:2, one launch (start us, length us, event | category | flops | bytes accessed | tf_op | source)
XLA Modules:
  0.0 558.9 jit_solution(8384365809282588198)
XLA Ops:
  8.7 90.5 %all-gather.7.cloned.1.call-done = bf16[2048,512]{1,0:T(8,128)(2,1)} async-done(((bf16[64,512]{1,0:T(8,128)(2,1)}), bf16[2048,512]{1,0:T(8,128)(2,1)}) %all-gather.7.cloned.1.call-update) | async-done | bytes 2097168 | tf_op jit(solution)/shard_map/all_gather | solution.py:107
  99.3 6.9 %all-to-all-start = ((bf16[4,512,512]{2,1,0:T(8,128)(2,1)}), bf16[4,512,512]{2,1,0:T(8,128)(2,1)S(1)}, u32[]{:S(2)}, u32[]{:S(2)}) async-start(bf16[4,512,512]{2,1,0:T(8,128)(2,1)} %bitcast.155), calls=%async_computation | async-start | bytes 4194304 | tf_op jit(solution)/shard_map/all_to_all | solution.py:112
  106.8 2.9 collective-permute-start
  109.7 3.3 collective-permute-start.1
  113.9 52.4 %all_gather.15 = bf16[32,8,512]{2,1,0:T(8,128)(2,1)S(1)} all-gather(bf16[1,8,512]{2,1,0:T(8,128)(2,1)S(1)} %slice.89), channel_id=1, replica_groups=mesh['dp'=4,'fsdp'=32,'head'=4] {'fsdp'}, dimensions={0}, use_global_device_ids=true | all-gather | bytes 270336 | tf_op jit(solution)/shard_map/all_gather | solution.py:75
  166.4 48.0 %all_gather.16 = bf16[32,8,512]{2,1,0:T(8,128)(2,1)S(1)} all-gather(bf16[1,8,512]{2,1,0:T(8,128)(2,1)S(1)} %slice.91), channel_id=1, replica_groups=mesh['dp'=4,'fsdp'=32,'head'=4] {'fsdp'}, dimensions={0}, use_global_device_ids=true | all-gather | bytes 270336 | tf_op jit(solution)/shard_map/all_gather | solution.py:74
  223.7 2.2 copy.103
  230.3 3.3 fusion.35
  233.6 2.4 copy.113
  235.9 2.7 convolution_convert_fusion.2
  241.2 27.9 %all-gather.5.cloned.1.call-done = bf16[256,2048]{1,0:T(8,128)(2,1)} async-done(((bf16[256,512]{1,0:T(8,128)(2,1)}), bf16[256,2048]{1,0:T(8,128)(2,1)}) %all-gather.5.cloned.1.call-update) | async-done | bytes 1048592 | tf_op jit(solution)/shard_map/all_gather | solution.py:106
  269.1 3.3 convolution_convert_fusion
  272.4 2.1 fusion.32
  274.5 1.4 copy-done.5
  276.8 1.5 slice.125
  281.5 10.6 %all-to-all-start.2 = ((bf16[32,8,512]{2,1,0:T(8,128)(2,1)}), bf16[32,8,512]{2,1,0:T(8,128)(2,1)}, u32[]{:S(2)}, u32[]{:S(2)}) async-start(bf16[32,8,512]{2,1,0:T(8,128)(2,1)} %copy.138), calls=%async_computation.2 | async-start | bytes 524288 | tf_op jit(solution)/shard_map/all_to_all | solution.py:156
  293.1 4.9 collective-permute-start.3
  298.7 1.8 multiply_bitcast_fusion
  300.5 1.9 copy.124
  302.4 1.3 slice.116
  303.7 3.0 copy.125
  306.8 1.6 slice_bitcast_fusion.5
  312.2 3.3 collective-permute-start.2
  317.9 1.8 bitcast_add_fusion
  319.8 6.8 %all-to-all-start.1 = ((bf16[32,8,512]{2,1,0:T(8,128)(2,1)}), bf16[32,8,512]{2,1,0:T(8,128)(2,1)S(1)}, u32[]{:S(2)}, u32[]{:S(2)}) async-start(bf16[32,8,512]{2,1,0:T(8,128)(2,1)} %copy.130), calls=%async_computation.1 | async-start | bytes 524288 | tf_op jit(solution)/shard_map/all_to_all | solution.py:149
  326.7 1.3 slice.152
  331.3 6.3 %all-to-all-done.1 = bf16[32,8,512]{2,1,0:T(8,128)(2,1)S(1)} async-done(((bf16[32,8,512]{2,1,0:T(8,128)(2,1)}), bf16[32,8,512]{2,1,0:T(8,128)(2,1)S(1)}, u32[]{:S(2)}, u32[]{:S(2)}) %all-to-all-start.1) | async-done | bytes 262176 | tf_op jit(solution)/shard_map/all_to_all | solution.py:149
  338.4 1.7 pad_maximum_fusion.7
  340.1 157.6 %reduce-scatter.2.cloned.1.call-done = bf16[64,512]{1,0:T(8,128)(2,1)} async-done(((bf16[2048,512]{1,0:T(8,128)(2,1)}), bf16[64,512]{1,0:T(8,128)(2,1)}) %reduce-scatter.2.cloned.1.call-update) | async-done | bytes 65552 | tf_op jit(solution)/shard_map/reduce_scatter | solution.py:177
  497.7 1.4 fusion.6
  499.1 50.7 %all-reduce.8.cloned.1.call-done = bf16[64,512]{1,0:T(8,128)(2,1)} async-done(((bf16[64,512]{1,0:T(8,128)(2,1)}), bf16[64,512]{1,0:T(8,128)(2,1)}) %all-reduce.8.cloned.1.call-update) | async-done | bytes 65552 | tf_op jit(solution)/shard_map/psum | solution.py:185
  549.9 1.5 convert_element_type.125
  (126 shorter events, 34.3 us)
Async XLA Ops:
  8.0 91.3 %all-gather.7.cloned.1.call-start = ((), (), s32[]{:S(2)}) async-start(), calls=%async_computation.5 | async-start | bytes 2162688 | tf_op jit(solution)/shard_map/all_gather | solution.py:107
  99.3 7.5 %copy-start.8 = (bf16[1,256,512]{2,1,0:T(8,128)(2,1)S(1)}, bf16[1,256,512]{2,1,0:T(8,128)(2,1)}, u32[]{:S(2)}) copy-start(bf16[1,256,512]{2,1,0:T(8,128)(2,1)} %param.8) | copy-start | bytes 786436
  99.3 10.4 %copy-start.9 = (bf16[1,256,512]{2,1,0:T(8,128)(2,1)S(1)}, bf16[1,256,512]{2,1,0:T(8,128)(2,1)}, u32[]{:S(2)}) copy-start(bf16[1,256,512]{2,1,0:T(8,128)(2,1)} %param.7) | copy-start | bytes 786436
  99.3 13.7 %copy-start.20 = (s32[1,2,16]{2,1,0:T(2,128)S(1)}, s32[1,2,16]{2,1,0:T(2,128)}, u32[]{:S(2)}) copy-start(s32[1,2,16]{2,1,0:T(2,128)} %param.10) | copy-start | bytes 388
  99.3 134.3 %all-to-all-start = ((bf16[4,512,512]{2,1,0:T(8,128)(2,1)}), bf16[4,512,512]{2,1,0:T(8,128)(2,1)S(1)}, u32[]{:S(2)}, u32[]{:S(2)}) async-start(bf16[4,512,512]{2,1,0:T(8,128)(2,1)} %bitcast.155), calls=%async_computation | async-start | bytes 4194304 | tf_op jit(solution)/shard_map/all_to_all | solution.py:112
  106.1 129.8 %all-gather.9.cloned.1.call-start = ((), (), s32[]{:S(2)}) async-start(), calls=%async_computation.8 | async-start | bytes 1310720 | tf_op jit(solution)/shard_map/all_gather | solution.py:111
  106.7 162.4 %all-gather.5.cloned.1.call-start = ((), (), s32[]{:S(2)}) async-start(), calls=%async_computation.4 | async-start | bytes 1310720 | tf_op jit(solution)/shard_map/all_gather | solution.py:106
  106.8 114.1 %collective-permute-start = (bf16[256,512]{1,0:T(8,128)(2,1)S(1)}, bf16[256,512]{1,0:T(8,128)(2,1)S(1)}, u32[]{:S(2)}, u32[]{:S(2)}) collective-permute-start(bf16[256,512]{1,0:T(8,128)(2,1)S(1)} %bitcast.163), channel_id=1, source_target_pairs={{0,4},{4,8},{8,12},{12,16},{16,20},{20,24},{24,28},{28,32},{32,36}... | collective-permute-start | bytes 786440 | tf_op jit(solution)/shard_map/ppermute | solution.py:18
  109.7 116.2 %collective-permute-start.1 = (bf16[256,512]{1,0:T(8,128)(2,1)S(1)}, bf16[256,512]{1,0:T(8,128)(2,1)}, u32[]{:S(2)}, u32[]{:S(2)}) collective-permute-start(bf16[256,512]{1,0:T(8,128)(2,1)S(1)} %bitcast.166), channel_id=1, source_target_pairs={{0,4},{4,8},{8,12},{12,16},{16,20},{20,24},{24,28},{28,32},{32,36}... | collective-permute-start | bytes 786440 | tf_op jit(solution)/shard_map/ppermute | solution.py:18
  227.8 2.4 copy-start.12
  230.3 42.1 %copy-start.1 = (bf16[2,512,4,128]{3,1,2,0:T(8,128)(2,1)}, bf16[2,512,4,128]{3,1,2,0:T(8,128)(2,1)S(1)}, u32[]{:S(2)}) copy-start(bf16[2,512,4,128]{3,1,2,0:T(8,128)(2,1)S(1)} %copy_dynamic-update-slice_fusion.1) | copy-start | bytes 3145732
  235.9 3.0 copy-start.13
  235.9 3.0 copy-start.14
  235.9 3.0 copy-start.16
  239.0 30.1 %copy-start.10 = (bf16[1,256,512]{2,1,0:T(8,128)(2,1)S(1)}, bf16[1,256,512]{2,1,0:T(8,128)(2,1)}, u32[]{:S(2)}) copy-start(bf16[1,256,512]{2,1,0:T(8,128)(2,1)} %param.11) | copy-start | bytes 786436
  241.2 256.5 %reduce-scatter.2.cloned.1.call-start = ((), (), s32[]{:S(2)}) async-start(), calls=%async_computation.6 | async-start | bytes 2162688 | tf_op jit(solution)/shard_map/reduce_scatter | solution.py:177
  281.5 38.3 %all-to-all-start.2 = ((bf16[32,8,512]{2,1,0:T(8,128)(2,1)}), bf16[32,8,512]{2,1,0:T(8,128)(2,1)}, u32[]{:S(2)}, u32[]{:S(2)}) async-start(bf16[32,8,512]{2,1,0:T(8,128)(2,1)} %copy.138), calls=%async_computation.2 | async-start | bytes 524288 | tf_op jit(solution)/shard_map/all_to_all | solution.py:156
  292.0 6.0 %copy-start.21 = (f32[2,4,128,512]{2,3,1,0:T(8,128)S(1)}, f32[2,4,128,512]{2,3,1,0:T(8,128)}, u32[]{:S(2)}) copy-start(f32[2,4,128,512]{2,3,1,0:T(8,128)} %get-tuple-element.12) | copy-start | bytes 6291460
  292.2 5.9 %copy-start.15 = (bf16[2,384,4,128]{1,3,2,0:T(8,128)(2,1)S(1)}, bf16[2,384,4,128]{1,3,2,0:T(8,128)(2,1)}, u32[]{:S(2)}) copy-start(bf16[2,384,4,128]{1,3,2,0:T(8,128)(2,1)} %copy.103) | copy-start | bytes 2359300
  292.2 5.9 %copy-start.17 = (bf16[2,128,4,128]{1,3,2,0:T(8,128)(2,1)S(1)}, bf16[2,128,4,128]{1,3,2,0:T(8,128)(2,1)}, u32[]{:S(2)}) copy-start(bf16[2,128,4,128]{1,3,2,0:T(8,128)(2,1)} %copy.104) | copy-start | bytes 786436
  292.2 5.9 %copy-start.19 = (bf16[2,128,4,128]{1,3,2,0:T(8,128)(2,1)S(1)}, bf16[2,128,4,128]{1,3,2,0:T(8,128)(2,1)}, u32[]{:S(2)}) copy-start(bf16[2,128,4,128]{1,3,2,0:T(8,128)(2,1)} %copy-done.18) | copy-start | bytes 786436
  292.4 5.6 %copy-start.3 = (f32[4,128,512]{2,1,0:T(8,128)}, f32[4,128,512]{2,1,0:T(8,128)S(1)}, u32[]{:S(2)}) copy-start(f32[4,128,512]{2,1,0:T(8,128)S(1)} %pad_add_fusion) | copy-start | bytes 3145732
  293.1 24.8 %collective-permute-start.3 = (bf16[256,512]{1,0:T(8,128)(2,1)}, bf16[256,512]{1,0:T(8,128)(2,1)}, u32[]{:S(2)}, u32[]{:S(2)}) collective-permute-start(bf16[256,512]{1,0:T(8,128)(2,1)} %bitcast.46), channel_id=1, source_target_pairs={{4,0},{8,4},{12,8},{16,12},{20,16},{24,20},{28,24},{32,28},{36,32}... | collective-permute-start | bytes 786440 | tf_op jit(solution)/shard_map/ppermute | solution.py:18
  306.8 1.7 copy-start.2
  309.1 6.9 %copy-start.4 = (f32[4,128,512]{2,1,0:T(8,128)}, f32[4,128,512]{2,1,0:T(8,128)S(1)}, u32[]{:S(2)}) copy-start(f32[4,128,512]{2,1,0:T(8,128)S(1)} %pad_add_fusion.1) | copy-start | bytes 3145732
  312.2 14.5 %collective-permute-start.2 = (bf16[256,512]{1,0:T(8,128)(2,1)}, bf16[256,512]{1,0:T(8,128)(2,1)S(1)}, u32[]{:S(2)}, u32[]{:S(2)}) collective-permute-start(bf16[256,512]{1,0:T(8,128)(2,1)} %bitcast.32), channel_id=1, source_target_pairs={{4,0},{8,4},{12,8},{16,12},{20,16},{24,20},{28,24},{32,28},{36,32}... | collective-permute-start | bytes 786440 | tf_op jit(solution)/shard_map/ppermute | solution.py:18
  315.5 2.4 slice-start
  316.0 10.6 %slice-start.1 = ((f32[4,128,512]{2,1,0:T(8,128)}), f32[2,128,512]{2,1,0:T(8,128)S(1)}, s32[]{:S(2)}) async-start(f32[4,128,512]{2,1,0:T(8,128)} %copy-done.4), calls=%async_computation.10 | async-start | bytes 1048576 | tf_op jit(solution)/shard_map/slice | solution.py:166
  319.8 17.9 %all-to-all-start.1 = ((bf16[32,8,512]{2,1,0:T(8,128)(2,1)}), bf16[32,8,512]{2,1,0:T(8,128)(2,1)S(1)}, u32[]{:S(2)}, u32[]{:S(2)}) async-start(bf16[32,8,512]{2,1,0:T(8,128)(2,1)} %copy.130), calls=%async_computation.1 | async-start | bytes 524288 | tf_op jit(solution)/shard_map/all_to_all | solution.py:149
  326.6 171.1 %copy-start = (bf16[256,2048]{1,0:T(8,128)(2,1)S(1)}, bf16[256,2048]{1,0:T(8,128)(2,1)}, u32[]{:S(2)}) copy-start(bf16[256,2048]{1,0:T(8,128)(2,1)} %all-gather.5.cloned.1.call-done) | copy-start | bytes 3145732
  326.6 223.3 %all-reduce.8.cloned.1.call-start = ((), (), s32[]{:S(2)}) async-start(), calls=%async_computation.7 | async-start | bytes 131072 | tf_op jit(solution)/shard_map/psum | solution.py:185
  326.7 171.0 %copy-start.6 = (bf16[2048,512]{1,0:T(8,128)(2,1)S(1)}, bf16[2048,512]{1,0:T(8,128)(2,1)}, u32[]{:S(2)}) copy-start(bf16[2048,512]{1,0:T(8,128)(2,1)} %all-gather.7.cloned.1.call-done) | copy-start | bytes 6291460
  (4 other events, 4.7 us)
Sparse Core Ops, SparseCore 0:
  12.0 87.2 all-gather.6
  272.5 225.0 reduce-scatter.1
Sparse Core Ops, SparseCore 1:
  108.7 40.2 all-gather.8
  241.2 27.8 all-gather.4
  497.8 52.0 all-reduce.7
where the time goes:
time: 560 us; the launch traced here: 559 us
  waiting for transfers between devices  334 us (60%)
  blocking collectives  100 us (18%)
  local copies, waits for them, and re-layouts  39 us (7%)
  starting transfers between devices  38.8 us (7%)
  matrix products  17.8 us (3%)
  between operations  16.3 us (3%)
  other arithmetic  12.2 us (2%)
    reduce_scatter x1, waiting for transfers between devices, body(): lax.psum_scatter(lax.dot_general(all_mixed, grad_tok, (((0,), (0,)), ((),...  158 us
    all_gather x1, waiting for transfers between devices, body(): weight_cols = lax.all_gather(out_weight, 'fsdp', axis=0, tiled=True)  90.5 us
    all_gather x1, blocking collectives, body(): lax.all_gather(tail_values, 'fsdp', axis=0, tiled=True)  52.4 us
    psum x1, waiting for transfers between devices, body(): weight_grad = lax.psum(shard_rows, 'dp').astype(jnp.float32)  50.7 us
    all_gather x1, blocking collectives, body(): lax.all_gather(tail_keys, 'fsdp', axis=0, tiled=True)  48 us
    all_gather x1, waiting for transfers between devices, body(): all_mixed = lax.all_gather(mixed, 'head', axis=1, tiled=True)  27.9 us
    ppermute x4, starting transfers between devices, shifted(): return lax.ppermute(block, axis, route)  14.4 us
  transfers between devices with their start and end apart: 12, of which 5 were waited for; matrix products, arithmetic and copies ran while one was open for 10% of the time, Pallas kernels for 0%

commit v1 on v0

--- a/solution.py
+++ b/solution.py
@@ -182,7 +182,7 @@
         scatter_dimension=0,
         tiled=True,
     )
-    weight_grad = lax.psum(shard_rows, "dp").astype(jnp.float32)
+    weight_grad = jnp.sum(lax.all_gather(shard_rows, "dp"), axis=0).astype(jnp.float32)
     return (projected[None], query_grad[None], key_grad[None], value_grad[None], weight_grad)
 
 

time: 560 us -> 521 us (0.930)
  the two profiles are of different devices: /device:TPU:2 before, /device:TPU:8 now
where the time goes in v1:
time: 521 us; the launch traced here: 520 us
  waiting for transfers between devices  290 us (56%)
  blocking collectives  113 us (22%)
  starting transfers between devices  38.1 us (7%)
  local copies, waits for them, and re-layouts  34.9 us (7%)
  matrix products  19.3 us (4%)
  between operations  16.1 us (3%)
  other arithmetic  9.26 us (2%)
    reduce_scatter x1, waiting for transfers between devices, body(): lax.psum_scatter(lax.dot_general(all_mixed, grad_tok, (((0,), (0,)), ((),...  156 us
    all_gather x1, waiting for transfers between devices, body(): weight_cols = lax.all_gather(out_weight, 'fsdp', axis=0, tiled=True)  91.9 us
    all_gather x1, blocking collectives, body(): lax.all_gather(tail_values, 'fsdp', axis=0, tiled=True)  50.7 us
    all_gather x1, blocking collectives, body(): lax.all_gather(tail_keys, 'fsdp', axis=0, tiled=True)  47.8 us
    all_gather x1, waiting for transfers between devices, body(): all_mixed = lax.all_gather(mixed, 'head', axis=1, tiled=True)  31.4 us
    all_gather x1, blocking collectives, body(): lax.all_gather(shard_rows, 'dp')  14 us
    all_to_all x1, starting transfers between devices, body(): lax.all_to_all(owner_rows(key_terms, selector, fsdp_count, stride_count)....  12.1 us
  transfers between devices with their start and end apart: 11, of which 4 were waited for; matrix products, arithmetic and copies ran while one was open for 10% of the time, Pallas kernels for 0%

profile of v1, /device:TPU:8, one launch (start us, length us, event | category | flops | bytes accessed | tf_op | source)
XLA Modules:
  0.0 520.3 jit_solution(7389945739418354270)
XLA Ops:
  8.7 91.9 %all-gather.8.cloned.1.call-done = bf16[2048,512]{1,0:T(8,128)(2,1)} async-done(((bf16[64,512]{1,0:T(8,128)(2,1)}), bf16[2048,512]{1,0:T(8,128)(2,1)}) %all-gather.8.cloned.1.call-update) | async-done | bytes 2097168 | tf_op jit(solution)/shard_map/all_gather | solution.py:107
  100.6 6.0 %all-to-all-start = ((bf16[4,512,512]{2,1,0:T(8,128)(2,1)}), bf16[4,512,512]{2,1,0:T(8,128)(2,1)S(1)}, u32[]{:S(2)}, u32[]{:S(2)}) async-start(bf16[4,512,512]{2,1,0:T(8,128)(2,1)} %bitcast.156), calls=%async_computation | async-start | bytes 4194304 | tf_op jit(solution)/shard_map/all_to_all | solution.py:112
  107.2 2.6 collective-permute-start
  109.8 4.2 collective-permute-start.1
  114.9 50.7 %all_gather.21 = bf16[32,8,512]{2,1,0:T(8,128)(2,1)S(1)} all-gather(bf16[1,8,512]{2,1,0:T(8,128)(2,1)S(1)} %slice.89), channel_id=1, replica_groups=mesh['dp'=4,'fsdp'=32,'head'=4] {'fsdp'}, dimensions={0}, use_global_device_ids=true | all-gather | bytes 270336 | tf_op jit(solution)/shard_map/all_gather | solution.py:75
  165.7 47.8 %all_gather.22 = bf16[32,8,512]{2,1,0:T(8,128)(2,1)S(1)} all-gather(bf16[1,8,512]{2,1,0:T(8,128)(2,1)S(1)} %slice.91), channel_id=1, replica_groups=mesh['dp'=4,'fsdp'=32,'head'=4] {'fsdp'}, dimensions={0}, use_global_device_ids=true | all-gather | bytes 270336 | tf_op jit(solution)/shard_map/all_gather | solution.py:74
  213.5 1.3 gather_fusion
  222.8 2.2 copy.103
  228.0 1.2 copy_dynamic-update-slice_fusion
  229.4 3.2 fusion.35
  232.6 2.3 copy.113
  235.0 2.7 convolution_convert_fusion.2
  238.0 1.2 multiply_reduce_fusion
  240.2 31.4 %all-gather.6.cloned.1.call-done = bf16[256,2048]{1,0:T(8,128)(2,1)} async-done(((bf16[256,512]{1,0:T(8,128)(2,1)}), bf16[256,2048]{1,0:T(8,128)(2,1)}) %all-gather.6.cloned.1.call-update) | async-done | bytes 1048592 | tf_op jit(solution)/shard_map/all_gather | solution.py:106
  271.6 3.3 convolution_convert_fusion
  274.9 2.1 fusion.32
  277.1 1.3 slice.125
  278.3 1.9 copy.151
  281.9 10.3 %all-to-all-start.2 = ((bf16[32,8,512]{2,1,0:T(8,128)(2,1)}), bf16[32,8,512]{2,1,0:T(8,128)(2,1)}, u32[]{:S(2)}, u32[]{:S(2)}) async-start(bf16[32,8,512]{2,1,0:T(8,128)(2,1)} %copy.138), calls=%async_computation.2 | async-start | bytes 524288 | tf_op jit(solution)/shard_map/all_to_all | solution.py:156
  293.3 1.6 collective-permute-start.3
  295.5 1.8 multiply_bitcast_fusion
  297.3 1.9 copy.124
  299.2 1.3 slice.116
  300.5 3.1 copy.125
  303.6 1.6 slice_bitcast_fusion.5
  306.9 1.2 copy.128
  309.0 1.3 collective-permute-start.2
  313.7 12.1 %all-to-all-start.1 = ((bf16[32,8,512]{2,1,0:T(8,128)(2,1)}), bf16[32,8,512]{2,1,0:T(8,128)(2,1)S(1)}, u32[]{:S(2)}, u32[]{:S(2)}) async-start(bf16[32,8,512]{2,1,0:T(8,128)(2,1)} %copy.130), calls=%async_computation.1 | async-start | bytes 524288 | tf_op jit(solution)/shard_map/all_to_all | solution.py:149
  328.8 9.2 %all-to-all-done.1 = bf16[32,8,512]{2,1,0:T(8,128)(2,1)S(1)} async-done(((bf16[32,8,512]{2,1,0:T(8,128)(2,1)}), bf16[32,8,512]{2,1,0:T(8,128)(2,1)S(1)}, u32[]{:S(2)}, u32[]{:S(2)}) %all-to-all-start.1) | async-done | bytes 262176 | tf_op jit(solution)/shard_map/all_to_all | solution.py:149
  338.8 3.0 fusion.6
  341.8 156.3 %reduce-scatter.2.cloned.1.call-done = bf16[64,512]{1,0:T(8,128)(2,1)} async-done(((bf16[2048,512]{1,0:T(8,128)(2,1)}), bf16[64,512]{1,0:T(8,128)(2,1)}) %reduce-scatter.2.cloned.1.call-update) | async-done | bytes 65552 | tf_op jit(solution)/shard_map/reduce_scatter | solution.py:177
  498.1 14.0 %all-gather.1 = bf16[256,512]{1,0:T(8,128)(2,1)S(1)} all-gather(bf16[64,512]{1,0:T(8,128)(2,1)} %reduce-scatter.2.cloned.1.call-done), channel_id=3, replica_groups=mesh['dp'=4,'fsdp'=32,'head'=4] {'dp'}, dimensions={0}, use_global_device_ids=true | all-gather | bytes 327680 | tf_op jit(solution)/shard_map/all_gather | solution.py:185
  (119 shorter events, 28.3 us)
Async XLA Ops:
  8.0 92.6 %all-gather.8.cloned.1.call-start = ((), (), s32[]{:S(2)}) async-start(), calls=%async_computation.5 | async-start | bytes 2162688 | tf_op jit(solution)/shard_map/all_gather | solution.py:107
  100.6 6.6 %copy-start.5 = (bf16[1,256,512]{2,1,0:T(8,128)(2,1)S(1)}, bf16[1,256,512]{2,1,0:T(8,128)(2,1)}, u32[]{:S(2)}) copy-start(bf16[1,256,512]{2,1,0:T(8,128)(2,1)} %param.8) | copy-start | bytes 786436
  100.6 9.2 %copy-start.6 = (bf16[1,256,512]{2,1,0:T(8,128)(2,1)S(1)}, bf16[1,256,512]{2,1,0:T(8,128)(2,1)}, u32[]{:S(2)}) copy-start(bf16[1,256,512]{2,1,0:T(8,128)(2,1)} %param.7) | copy-start | bytes 786436
  100.6 13.4 %copy-start.17 = (s32[1,2,16]{2,1,0:T(2,128)S(1)}, s32[1,2,16]{2,1,0:T(2,128)}, u32[]{:S(2)}) copy-start(s32[1,2,16]{2,1,0:T(2,128)} %param.10) | copy-start | bytes 388
  100.6 132.0 %all-to-all-start = ((bf16[4,512,512]{2,1,0:T(8,128)(2,1)}), bf16[4,512,512]{2,1,0:T(8,128)(2,1)S(1)}, u32[]{:S(2)}, u32[]{:S(2)}) async-start(bf16[4,512,512]{2,1,0:T(8,128)(2,1)} %bitcast.156), calls=%async_computation | async-start | bytes 4194304 | tf_op jit(solution)/shard_map/all_to_all | solution.py:112
  106.6 128.4 %all-gather.10.cloned.1.call-start = ((), (), s32[]{:S(2)}) async-start(), calls=%async_computation.7 | async-start | bytes 1310720 | tf_op jit(solution)/shard_map/all_gather | solution.py:111
  107.1 164.5 %all-gather.6.cloned.1.call-start = ((), (), s32[]{:S(2)}) async-start(), calls=%async_computation.4 | async-start | bytes 1310720 | tf_op jit(solution)/shard_map/all_gather | solution.py:106
  107.2 112.7 %collective-permute-start = (bf16[256,512]{1,0:T(8,128)(2,1)S(1)}, bf16[256,512]{1,0:T(8,128)(2,1)S(1)}, u32[]{:S(2)}, u32[]{:S(2)}) collective-permute-start(bf16[256,512]{1,0:T(8,128)(2,1)S(1)} %bitcast.164), channel_id=1, source_target_pairs={{0,4},{4,8},{8,12},{12,16},{16,20},{20,24},{24,28},{28,32},{32,36}... | collective-permute-start | bytes 786440 | tf_op jit(solution)/shard_map/ppermute | solution.py:18
  109.8 115.2 %collective-permute-start.1 = (bf16[256,512]{1,0:T(8,128)(2,1)S(1)}, bf16[256,512]{1,0:T(8,128)(2,1)}, u32[]{:S(2)}, u32[]{:S(2)}) collective-permute-start(bf16[256,512]{1,0:T(8,128)(2,1)S(1)} %bitcast.167), channel_id=1, source_target_pairs={{0,4},{4,8},{8,12},{12,16},{16,20},{20,24},{24,28},{28,32},{32,36}... | collective-permute-start | bytes 786440 | tf_op jit(solution)/shard_map/ppermute | solution.py:18
  219.9 0.7 copy-start.8
  226.9 2.4 copy-start.9
  229.4 45.5 %copy-start.1 = (bf16[2,512,4,128]{3,1,2,0:T(8,128)(2,1)}, bf16[2,512,4,128]{3,1,2,0:T(8,128)(2,1)S(1)}, u32[]{:S(2)}) copy-start(bf16[2,512,4,128]{3,1,2,0:T(8,128)(2,1)S(1)} %copy_dynamic-update-slice_fusion.1) | copy-start | bytes 3145732
  235.0 3.0 copy-start.10
  235.0 3.0 copy-start.11
  235.0 3.0 copy-start.13
  238.0 1.3 copy-start.15
  238.0 33.6 %copy-start.7 = (bf16[1,256,512]{2,1,0:T(8,128)(2,1)S(1)}, bf16[1,256,512]{2,1,0:T(8,128)(2,1)}, u32[]{:S(2)}) copy-start(bf16[1,256,512]{2,1,0:T(8,128)(2,1)} %param.11) | copy-start | bytes 786436
  240.2 257.9 %reduce-scatter.2.cloned.1.call-start = ((), (), s32[]{:S(2)}) async-start(), calls=%async_computation.6 | async-start | bytes 2162688 | tf_op jit(solution)/shard_map/reduce_scatter | solution.py:177
  281.9 31.9 %all-to-all-start.2 = ((bf16[32,8,512]{2,1,0:T(8,128)(2,1)}), bf16[32,8,512]{2,1,0:T(8,128)(2,1)}, u32[]{:S(2)}, u32[]{:S(2)}) async-start(bf16[32,8,512]{2,1,0:T(8,128)(2,1)} %copy.138), calls=%async_computation.2 | async-start | bytes 524288 | tf_op jit(solution)/shard_map/all_to_all | solution.py:156
  292.2 2.7 copy-start.18
  292.3 2.6 copy-start.12
  292.3 2.6 copy-start.14
  292.3 2.6 copy-start.16
  292.5 3.0 copy-start.3
  293.3 19.4 %collective-permute-start.3 = (bf16[256,512]{1,0:T(8,128)(2,1)}, bf16[256,512]{1,0:T(8,128)(2,1)}, u32[]{:S(2)}, u32[]{:S(2)}) collective-permute-start(bf16[256,512]{1,0:T(8,128)(2,1)} %bitcast.46), channel_id=1, source_target_pairs={{4,0},{8,4},{12,8},{16,12},{20,16},{24,20},{28,24},{32,28},{36,32}... | collective-permute-start | bytes 786440 | tf_op jit(solution)/shard_map/ppermute | solution.py:18
  303.6 1.7 copy-start.2
  305.9 4.8 copy-start.4
  309.0 16.8 %collective-permute-start.2 = (bf16[256,512]{1,0:T(8,128)(2,1)}, bf16[256,512]{1,0:T(8,128)(2,1)}, u32[]{:S(2)}, u32[]{:S(2)}) collective-permute-start(bf16[256,512]{1,0:T(8,128)(2,1)} %bitcast.32), channel_id=1, source_target_pairs={{4,0},{8,4},{12,8},{16,12},{20,16},{24,20},{28,24},{32,28},{36,32}... | collective-permute-start | bytes 786440 | tf_op jit(solution)/shard_map/ppermute | solution.py:18
  310.3 2.4 slice-start
  310.8 15.1 %slice-start.1 = ((f32[4,128,512]{2,1,0:T(8,128)}), f32[2,128,512]{2,1,0:T(8,128)S(1)}, s32[]{:S(2)}) async-start(f32[4,128,512]{2,1,0:T(8,128)} %copy-done.4), calls=%async_computation.9 | async-start | bytes 1048576 | tf_op jit(solution)/shard_map/slice | solution.py:166
  313.7 24.3 %all-to-all-start.1 = ((bf16[32,8,512]{2,1,0:T(8,128)(2,1)}), bf16[32,8,512]{2,1,0:T(8,128)(2,1)S(1)}, u32[]{:S(2)}, u32[]{:S(2)}) async-start(bf16[32,8,512]{2,1,0:T(8,128)(2,1)} %copy.130), calls=%async_computation.1 | async-start | bytes 524288 | tf_op jit(solution)/shard_map/all_to_all | solution.py:149
  325.8 13.0 %copy-start = (bf16[256,2048]{1,0:T(8,128)(2,1)S(1)}, bf16[256,2048]{1,0:T(8,128)(2,1)}, u32[]{:S(2)}) copy-start(bf16[256,2048]{1,0:T(8,128)(2,1)} %all-gather.6.cloned.1.call-done) | copy-start | bytes 3145732
Sparse Core Ops, SparseCore 0:
  12.0 88.5 all-gather.7
  275.0 223.0 reduce-scatter.1
Sparse Core Ops, SparseCore 1:
  109.1 45.5 all-gather.9
  240.3 31.3 all-gather.5
